TPU v7x, 256 devices: a whole 4x4x8 slice. The times are simulated.
256 devices in a mesh: section: 16 (over y_hi, z), fsdp: 16 (over y_lo, x, core).
Axes of the slice: x: 4, y: 4 (y_hi: 2, y_lo: 2; y = y_hi * 2 + y_lo), z: 8, core: 2. Of those that a mesh axis runs over, the one named last changes fastest.
Arguments:
- patch_rows: bfloat16 [16, 2048, 1280], P('section', 'fsdp'), may hold values from -6 to 6
- query: bfloat16 [16, 2048, 640], P('section', 'fsdp'), may hold values from -32 to 32
- key_rows: bfloat16 [16, 2048, 640], P('section', 'fsdp'), may hold values from -32 to 32
- value_rows: bfloat16 [16, 2048, 640], P('section', 'fsdp'), may hold values from -6 to 6
- image_lengths: int32 [16, 4], P('section'), may hold values from 1 to 256, 512 in all within a row
- token_slots: int32 [16, 512], P('section', 'fsdp'), may hold values from 0 to 2047, as said below
- out_proj: bfloat16 [640, 1280], P('fsdp'), may hold values from -0.25 to 0.25
- merge_gain: float32 [1280], replicated, may hold values from 0.1 to 1.9
- merger_weight: bfloat16 [5120, 4096], P('section', 'fsdp'), may hold values from -0.078125 to 0.078125
- text_rows: bfloat16 [16, 2048, 4096], P('section', 'fsdp'), may hold values from -6 to 6
- norm_gain: float32 [4096], replicated, may hold values from 0.1 to 1.9
- out_grad: bfloat16 [16, 2048, 4096], P('section', 'fsdp'), may hold values from -6 to 6
Outputs:
- llm_input: bfloat16 [16, 2048, 4096], P('section', 'fsdp')
- grad_patches: bfloat16 [16, 2048, 1280], P('section', 'fsdp')
- grad_query: bfloat16 [16, 2048, 640], P('section', 'fsdp')
- grad_key: bfloat16 [16, 2048, 640], P('section', 'fsdp')
- grad_value: bfloat16 [16, 2048, 640], P('section', 'fsdp')
- grad_norm_gain: float32 [4096], replicated
- grad_merge_gain: float32 [1280], replicated
- grad_merger: float32 [5120, 4096], P('section', 'fsdp')
- grad_out_proj: float32 [640, 1280], P('fsdp')
Inputs may be any that keep to these rules, and one draw needn't show every extreme that they name: `token_slots`: within a micro-batch the values are distinct, and every block of 128 consecutive token rows receives exactly 32 of them.
All inputs are finite; a program needn't handle non-finite values.
Results may differ from a plain program's by a relative error of at most 0.03.
Values may be sent and summed in bfloat16 or wider, within the bound.
No kernel may reach another device: no remote copies, remote signals or barrier semaphores. Data moves between devices by JAX's collectives and lax.ppermute only.
A program may use at most 128 MiB of HBM per device.

v0:
```python
import jax
import jax.numpy as jnp
from jax import lax
from jax.sharding import Mesh
from jax.sharding import PartitionSpec as P

HEAD_DIM = 80
FSDP = ("fsdp_0", "fsdp_1", "fsdp_2")
SECTION = ("section_0", "section_1")
SECTION_FSDP = ("section_0", "section_1", "fsdp_0", "fsdp_1", "fsdp_2")
EPS = 1e-06


def sent_together(arrays, axis, dim, along):
    widths = [a.shape[along] for a in arrays]
    both = jnp.concatenate(arrays, axis=along)
    result = lax.all_gather(both, axis, axis=dim, tiled=True)
    return tuple(jnp.split(result, [sum(widths[:k]) for k in range(1, len(widths))], axis=along))


def in_order(pieces, dim):
    dims = list(pieces.shape[1:])
    dims[dim] *= pieces.shape[0]
    return jnp.moveaxis(pieces, 0, dim).reshape(dims)


def sent_to_all(x, axis):
    copies = jnp.broadcast_to(x, (lax.axis_size(axis), *x.shape))
    return lax.all_to_all(copies, axis, split_axis=0, concat_axis=0, tiled=True)


def gathered_copies(x, axis, dim):
    return in_order(sent_to_all(x, axis), dim)


def in_blocks(x, dim, count):
    dims = x.shape
    pieces = x.reshape(*dims[:dim], count, dims[dim] // count, *dims[dim + 1 :])
    return jnp.moveaxis(pieces, dim, 0)


def sum_at_owner(x, axis, dim):
    pieces = in_blocks(x, dim, lax.axis_size(axis))
    arrived = lax.all_to_all(pieces, axis, split_axis=0, concat_axis=0, tiled=True)
    return arrived.astype(jnp.float32).sum(axis=0)


def reduced_to_own(pieces, axes, sequence):
    inside = pieces.shape[1:]
    pieces = pieces.reshape(*(lax.axis_size(a) for a in axes), *inside)
    pieces = jnp.moveaxis(pieces, sequence, range(len(axes))).reshape(-1, *inside)
    for k in sequence:
        pieces = lax.psum_scatter(pieces, axes[k], scatter_dimension=0, tiled=True)
    return pieces[0]


def summed_rows(x, axes, sequence, dim):
    count = lax.axis_size(axes)
    return reduced_to_own(in_blocks(x, dim, count), axes, sequence)


def over_copies(x, axis):
    return sent_to_all(x, axis).astype(jnp.float32).sum(axis=0)


def over_axes(x, axes):
    for axis in axes:
        x = lax.psum(x, axis)
    return x


def sent_together_2(arrays, axis, dim, along):
    ends, at = ([], 0)
    for a in arrays[:-1]:
        at += a.shape[along]
        ends.append(at)
    both = jnp.concatenate(arrays, axis=along)
    return tuple(
        jnp.split(lax.psum_scatter(both, axis, scatter_dimension=dim, tiled=True), ends, axis=along)
    )


def image_ids(ends, index):
    merged_index = index // 4
    return jnp.sum((merged_index[:, None] >= ends[None, :]).astype(jnp.int32), axis=1)


def split_heads(rows):
    return rows.reshape(rows.shape[0], -1, HEAD_DIM)


def whole_probs(query_heads, key_heads, mask):
    scale = HEAD_DIM ** (-0.5)
    scores = (
        jnp.einsum("qhd,khd->hqk", query_heads, key_heads, preferred_element_type=jnp.float32)
        * scale
    )
    scores = jnp.where(mask[None], scores, -jnp.inf)
    top = jnp.max(scores, axis=-1, keepdims=True)
    weights = jnp.where(mask[None], jnp.exp(scores - top), 0.0)
    return (weights / jnp.sum(weights, axis=-1, keepdims=True), scale)


def on_device(
    patch_rows,
    query,
    key_rows,
    value_rows,
    image_lengths,
    token_slots,
    out_proj,
    merge_gain,
    merger_weight,
    text_rows,
    norm_gain,
    out_grad,
):
    patches = patch_rows[0]
    rows, width = patches.shape
    att_width = query.shape[2]
    place = lax.axis_index(FSDP)
    groups = lax.axis_size(FSDP)
    ends = jnp.cumsum(image_lengths[0])
    own_index = place * rows + jnp.arange(rows, dtype=jnp.int32)
    all_index = jnp.arange(rows * groups, dtype=jnp.int32)
    mask = image_ids(ends, own_index)[:, None] == image_ids(ends, all_index)[None, :]
    keys_all, values_all = sent_together((key_rows[0], value_rows[0]), FSDP, 0, 1)
    query_heads = split_heads(query[0])
    key_heads = split_heads(keys_all)
    value_heads = split_heads(values_all)
    probs, scale = whole_probs(query_heads, key_heads, mask)
    probs_low = probs.astype(jnp.bfloat16)
    attended = jnp.einsum(
        "hqk,khd->qhd", probs_low, value_heads, preferred_element_type=jnp.float32
    )
    attended = attended.reshape(rows, att_width).astype(jnp.bfloat16)
    proj_full = gathered_copies(out_proj, FSDP, 0)
    mixed = patches.astype(jnp.float32) + jnp.dot(
        attended, proj_full, preferred_element_type=jnp.float32
    )
    centre = mixed - jnp.mean(mixed, axis=-1, keepdims=True)
    inv_std = lax.rsqrt(jnp.mean(centre * centre, axis=-1, keepdims=True) + EPS)
    unit = centre * inv_std
    normed = (unit * merge_gain).astype(jnp.bfloat16)
    merged_local = normed.reshape(rows // 4, 4 * width)
    merged_all, slots_all = (
        lax.all_gather(merged_local, FSDP, axis=0, tiled=True),
        lax.all_gather(token_slots[0], FSDP, axis=0, tiled=True),
    )
    merger_cols = lax.all_gather(merger_weight, SECTION, axis=0, tiled=True)
    projected = jnp.dot(merged_all, merger_cols, preferred_element_type=jnp.float32).astype(
        jnp.bfloat16
    )
    order = jnp.argsort(slots_all)
    inverse = jnp.argsort(order)
    sorted_slots = slots_all[order]
    mine = lax.all_to_all(projected[order], FSDP, split_axis=0, concat_axis=1, tiled=True)
    count = mine.shape[0]
    text = text_rows[0]
    tokens = text.shape[0]
    local_rows = lax.dynamic_slice_in_dim(sorted_slots, place * count, count) - place * tokens
    stream = text.at[local_rows].set(mine).astype(jnp.float32)
    inv_rms = lax.rsqrt(jnp.mean(stream * stream, axis=-1, keepdims=True) + EPS)
    scaled = stream * inv_rms
    llm_input = (scaled * norm_gain).astype(jnp.bfloat16)
    upstream_raw = out_grad[0].astype(jnp.float32)
    norm_gain_part = jnp.sum(upstream_raw * scaled, axis=0)
    upstream = upstream_raw * norm_gain
    stream_grad = inv_rms * (
        upstream - scaled * jnp.mean(upstream * scaled, axis=-1, keepdims=True)
    )
    image_grad = stream_grad[local_rows].astype(jnp.bfloat16)
    returned = lax.all_to_all(image_grad, FSDP, split_axis=1, concat_axis=0, tiled=True)[inverse]
    block = lax.slice_in_dim(returned, 0, merged_local.shape[0] * lax.axis_size(FSDP), axis=0)
    merged_grad = sum_at_owner(
        jnp.dot(block, merger_cols.T, preferred_element_type=jnp.float32).astype(jnp.bfloat16),
        FSDP,
        0,
    )
    block = merged_all
    merger_grad = summed_rows(
        jnp.dot(block.T, returned, preferred_element_type=jnp.float32).astype(jnp.bfloat16),
        SECTION,
        (1, 0),
        0,
    ).astype(jnp.float32)
    normed_grad = merged_grad.reshape(rows, width)
    merge_gain_part = jnp.sum(normed_grad * unit, axis=0)
    unit_grad = normed_grad * merge_gain
    mixed_grad = inv_std * (
        unit_grad
        - jnp.mean(unit_grad, axis=-1, keepdims=True)
        - unit * jnp.mean(unit_grad * unit, axis=-1, keepdims=True)
    )
    mixed_low = mixed_grad.astype(jnp.bfloat16)
    block = attended
    proj_part = sum_at_owner(
        jnp.dot(block.T, mixed_low, preferred_element_type=jnp.float32).astype(jnp.bfloat16),
        FSDP,
        0,
    )
    proj_grad = over_copies(proj_part.astype(jnp.bfloat16), SECTION).astype(jnp.float32)
    norm_total, merge_total = (
        over_axes(norm_gain_part, SECTION_FSDP),
        over_axes(merge_gain_part, SECTION_FSDP),
    )
    attended_grad = jnp.dot(mixed_low, proj_full.T, preferred_element_type=jnp.float32).astype(
        jnp.bfloat16
    )
    grad_heads = split_heads(attended_grad)
    value_grad = jnp.einsum(
        "hqk,qhd->khd", probs_low, grad_heads, preferred_element_type=jnp.float32
    )
    prob_grad = jnp.einsum(
        "qhd,khd->hqk", grad_heads, value_heads, preferred_element_type=jnp.float32
    )
    score_grad = probs * (prob_grad - jnp.sum(prob_grad * probs, axis=-1, keepdims=True))
    score_low = (score_grad * scale).astype(jnp.bfloat16)
    query_grad = jnp.einsum(
        "hqk,khd->qhd", score_low, key_heads, preferred_element_type=jnp.float32
    ).reshape(rows, att_width)
    key_grad = jnp.einsum(
        "hqk,qhd->khd", score_low, query_heads, preferred_element_type=jnp.float32
    )
    total_rows = key_grad.shape[0]
    key_own, value_own = tuple(
        (
            part.astype(jnp.float32)
            for part in sent_together_2(
                (
                    key_grad.reshape(total_rows, att_width).astype(jnp.bfloat16),
                    value_grad.reshape(total_rows, att_width).astype(jnp.bfloat16),
                ),
                FSDP,
                0,
                1,
            )
        )
    )
    return (
        llm_input[None],
        mixed_low[None],
        query_grad.astype(jnp.bfloat16)[None],
        key_own.astype(jnp.bfloat16)[None],
        value_own.astype(jnp.bfloat16)[None],
        norm_total,
        merge_total,
        merger_grad,
        proj_grad,
    )


def solution(mesh):
    torus = Mesh(
        mesh.devices.reshape(2, 8, 2, 4, 2),
        ("section_0", "section_1", "fsdp_0", "fsdp_1", "fsdp_2"),
    )
    placed = (
        P(SECTION, FSDP, None),
        P(SECTION, FSDP, None),
        P(SECTION, FSDP, None),
        P(SECTION, FSDP, None),
        P(SECTION, None),
        P(SECTION, FSDP),
        P(FSDP, None),
        P(),
        P(SECTION, FSDP),
        P(SECTION, FSDP, None),
        P(),
        P(SECTION, FSDP, None),
    )
    return jax.shard_map(
        on_device,
        mesh=torus,
        in_specs=placed,
        out_specs=(
            P(SECTION, FSDP, None),
            P(SECTION, FSDP, None),
            P(SECTION, FSDP, None),
            P(SECTION, FSDP, None),
            P(SECTION, FSDP, None),
            P(),
            P(),
            P(SECTION, FSDP),
            P(FSDP, None),
        ),
        check_vma=False,
    )
```

profile of v0, /device:TPU:1, one launch (start us, length us, event | category | flops | bytes accessed | tf_op | source)
XLA Modules:
  0.0 517.0 jit_solution(1756903741598296426)
XLA Ops:
  7.2 1.8 pad_maximum_fusion.1
  9.1 0.7 all-gather.9.cloned.1.call-update
  9.8 2.2 broadcast_in_dim.74
  12.0 6.8 %all-to-all-start = ((bf16[16,40,1280]{2,1,0:T(8,128)(2,1)}), bf16[16,40,1280]{2,1,0:T(8,128)(2,1)S(1)}, u32[]{:S(2)}, u32[]{:S(2)}) async-start(bf16[16,40,1280]{2,1,0:T(8,128)(2,1)} %broadcast_in_dim.74), calls=%async_computation | async-start | bytes 3276800 | tf_op jit(solution)/shard_map/all_to_all | solution.py:29
  19.4 0.3 broadcast_compare_fusion
  19.8 47.4 %all-gather.5.cloned.1.call-done = bf16[2048,1280]{1,0:T(8,128)(2,1)} async-done(((bf16[128,1280]{1,0:T(8,128)(2,1)}), bf16[2048,1280]{1,0:T(8,128)(2,1)}) %all-gather.5.cloned.1.call-update) | async-done | bytes 5242896 | tf_op jit(solution)/shard_map/all_gather | solution.py:17
  67.2 5.3 %fusion.48 = (bf16[2048,640]{1,0:T(8,128)(2,1)}, bf16[2048,640]{1,0:T(8,128)(2,1)}) fusion(bf16[2048,1280]{1,0:T(8,128)(2,1)} %all-gather.5.cloned.1.call-done), kind=kLoop, calls=%fused_computation.95 | loop fusion | bytes 10485760 | tf_op jit(solution)/shard_map/split | solution.py:18
  72.5 4.6 copy.72
  77.0 4.5 copy.71
  81.5 8.7 %fusion.49 = (f32[8,128]{1,0:T(8,128)S(1)}, f32[8,128,2048]{1,2,0:T(8,128)}) fusion(pred[128,2048]{0,1:T(8,128)(4,1)S(1)} %broadcast_compare_fusion, bf16[2048,8,80]{0,2,1:T(8,128)(2,1)} %bitcast.104, bf16[128,8,80]{0,2,1:T(8,128)(2,1)S(1)} %bitcast.118), kind=kOutput, calls=%fused_computation.96 | convolution fusion | flops 346032128 | bytes 11440128 | tf_op jit(solution)/shard_map/sub | solution.py:100
  90.2 5.2 %fusion.30 = bf16[8,80,128]{2,1,0:T(8,128)(2,1)S(1)} fusion(bf16[2048,8,80]{0,2,1:T(8,128)(2,1)} %bitcast.100, f32[8,128,2048]{1,2,0:T(8,128)} %get-tuple-element.70, f32[8,128]{1,0:T(8,128)S(1)} %get-tuple-element.69), kind=kOutput, calls=%fused_computation.45 | convolution fusion | flops 339820544 | bytes 11177984 | tf_op jit(solution)/shard_map/hqk,khd->qhd/dot_general | solution.py:133
  95.4 1.2 copy-done.1
  96.7 2.0 fusion.50
  99.1 0.9 reshape.203
  100.0 0.6 dynamic-slice
  101.4 8.4 %all-reduce = s32[512]{0:T(512)S(1)} all-reduce(s32[512]{0:T(512)S(1)} %bitcast_dynamic-update-slice_fusion), channel_id=2, replica_groups=mesh['section_0'=2,'section_1'=8,'fsdp_0'=2,'fsdp_1'=4,'fsdp_2'=2] {'fsd..., use_global_device_ids=true, to_apply=%add | all-reduce | flops 512 | bytes 4096 | tf_op jit(solution)/shard_map/all_gather | solution.py:148
  109.8 3.8 sort.31
  113.6 42.9 %all-gather.9.cloned.1.call-done = bf16[5120,256]{1,0:T(8,128)(2,1)} async-done(((bf16[320,256]{1,0:T(8,128)(2,1)}), bf16[5120,256]{1,0:T(8,128)(2,1)}) %all-gather.9.cloned.1.call-update) | async-done | bytes 2621456 | tf_op jit(solution)/shard_map/all_gather | solution.py:150
  156.5 44.9 %all-gather.7.cloned.1.call-done = bf16[512,5120]{1,0:T(8,128)(2,1)} async-done(((bf16[32,5120]{1,0:T(8,128)(2,1)}), bf16[512,5120]{1,0:T(8,128)(2,1)}) %all-gather.7.cloned.1.call-update) | async-done | bytes 5242896 | tf_op jit(solution)/shard_map/all_gather | solution.py:147
  201.4 4.8 convolution_convert_fusion.4
  206.2 2.6 gather_fusion.1
  208.8 3.8 all-to-all-start.1
  212.6 3.5 gather_fusion
  216.1 3.8 sort.32
  220.0 1.7 scatter_fusion
  221.7 0.3 fusion.25
  222.0 1.8 fusion.26
  223.9 0.6 fusion.22
  224.5 0.7 gather_fusion.2
  225.2 0.7 copy.95
  225.9 5.7 %all-to-all-start.2 = ((bf16[32,16,256]{2,0,1:T(8,128)(2,1)}), bf16[32,16,256]{2,0,1:T(8,128)(2,1)S(1)}, u32[]{:S(2)}, u32[]{:S(2)}) async-start(bf16[32,16,256]{2,0,1:T(8,128)(2,1)} %bitcast.92), calls=%async_computation.2 | async-start | bytes 524288 | tf_op jit(solution)/shard_map/all_to_all | solution.py:173
  231.6 7.2 %all-to-all-done.2 = bf16[32,16,256]{2,0,1:T(8,128)(2,1)S(1)} async-done(((bf16[32,16,256]{2,0,1:T(8,128)(2,1)}), bf16[32,16,256]{2,0,1:T(8,128)(2,1)S(1)}, u32[]{:S(2)}, u32[]{:S(2)}) %all-to-all-start.2) | async-done | bytes 262176 | tf_op jit(solution)/shard_map/all_to_all | solution.py:173
  238.8 1.9 gather_fusion.3
  240.8 5.7 %convolution_convert_fusion = bf16[512,5120]{1,0:T(8,128)(2,1)} fusion(bf16[512,256]{1,0:T(8,128)(2,1)S(1)} %gather_fusion.3, bf16[5120,256]{1,0:T(8,128)(2,1)} %all-gather.9.cloned.1.call-done), kind=kOutput, calls=%fused_computation.13 | convolution fusion | flops 1344798720 | bytes 8126464 | tf_op jit(solution)/shard_map/dot_general | solution.py:176
  246.5 5.1 all-to-all-start.3
  251.6 4.1 convolution_convert_fusion.1
  255.7 1.7 copy.85
  257.3 0.3 reduce-scatter.8.cloned.1.call-start
  257.6 63.6 %all-to-all-done.3 = bf16[16,32,5120]{2,1,0:T(8,128)(2,1)} async-done(((bf16[16,32,5120]{2,1,0:T(8,128)(2,1)}), bf16[16,32,5120]{2,1,0:T(8,128)(2,1)}, u32[]{:S(2)}, u32[]{:S(2)}) %all-to-all-start.3) | async-done | bytes 5242912 | tf_op jit(solution)/shard_map/all_to_all | solution.py:44
  321.2 3.5 convert_reduce_fusion
  324.9 0.3 multiply_reduce_fusion.1
  325.2 0.3 multiply_convert_fusion.1
  325.5 2.2 convolution_convert_fusion.5
  327.9 6.5 %convolution_convert_fusion.3 = bf16[8,80,2048]{2,1,0:T(8,128)(2,1)} fusion(bf16[128,8,80]{0,2,1:T(8,128)(2,1)S(1)} %bitcast.114, f32[8,128,2048]{1,2,0:T(8,128)} %get-tuple-element.70, f32[8,128]{1,0:T(8,128)S(1)} %get-tuple-element.69), kind=kOutput, calls=%fused_computation.26 | convolution fusion | flops 341049344 | bytes 11177984 | tf_op jit(solution)/shard_map/hqk,qhd->khd/dot_general | solution.py:211
  334.4 3.1 copy.84
  337.5 6.4 %fusion.51 = f32[8,128,2048]{1,2,0:T(8,128)} fusion(bf16[128,8,80]{0,2,1:T(8,128)(2,1)S(1)} %bitcast.115, bf16[2048,8,80]{0,2,1:T(8,128)(2,1)} %bitcast.101), kind=kOutput, calls=%fused_computation.98 | convolution fusion | flops 335544320 | bytes 11173888 | tf_op jit(solution)/shard_map/qhd,khd->hqk/dot_general | solution.py:214
  344.0 14.6 %fusion.15 = bf16[8,2048,80]{1,2,0:T(8,128)(2,1)} fusion(bf16[128,8,80]{0,2,1:T(8,128)(2,1)S(1)} %bitcast.119, f32[8,128,2048]{1,2,0:T(8,128)} %fusion.51, f32[8,128,2048]{1,2,0:T(8,128)} %get-tuple-element.70, f32[8,128]{1,0:T(8,128)S(1)} %get-tuple-element.69), kind=kOutput, calls=%fused_computation.24 | convolution fusion | flops 351538176 | bytes 19566592 | tf_op jit(solution)/shard_map/hqk,qhd->khd/dot_general | solution.py:222
  358.6 4.4 copy.83
  363.0 4.4 pad_maximum_fusion
  367.5 0.6 convolution_convert_fusion.2
  368.1 28.9 %all_to_all.55 = bf16[16,40,1280]{2,1,0:T(8,128)(2,1)S(1)} all-to-all(bf16[16,40,1280]{2,1,0:T(8,128)(2,1)S(1)} %bitcast.102), channel_id=1, replica_groups=mesh['section_0'=2,'section_1'=8,'fsdp_0'=2,'fsdp_1'=4,'fsdp_2'=2] {'fsd..., dimensions={0} | all-to-all | bytes 3276800 | tf_op jit(solution)/shard_map/all_to_all | solution.py:44
  396.9 0.3 reduce_sum.151
  397.2 1.3 broadcast_in_dim.80
  398.5 9.2 %all-to-all-start.5 = ((bf16[16,40,1280]{2,1,0:T(8,128)(2,1)}), bf16[16,40,1280]{2,1,0:T(8,128)(2,1)S(1)}, u32[]{:S(2)}, u32[]{:S(2)}) async-start(bf16[16,40,1280]{2,1,0:T(8,128)(2,1)} %broadcast_in_dim.80), calls=%async_computation.8 | async-start | bytes 3276800 | tf_op jit(solution)/shard_map/all_to_all | solution.py:29
  407.7 14.6 %fusion.33 = bf16[8,80,128]{2,1,0:T(8,128)(2,1)S(1)} fusion(bf16[2048,8,80]{0,2,1:T(8,128)(2,1)} %bitcast.105, f32[8,128,2048]{1,2,0:T(8,128)} %fusion.51, f32[8,128,2048]{1,2,0:T(8,128)} %get-tuple-element.70, f32[8,128]{1,0:T(8,128)S(1)} %get-tuple-element.69), kind=kOutput, calls=%fused_computation.46 | convolution fusion | flops 350309376 | bytes 19566592 | tf_op jit(solution)/shard_map/hqk,khd->qhd/dot_general | solution.py:219
  422.3 0.8 copy.86
  423.2 21.3 %all-reduce.5 = (f32[4096]{0:T(1024)S(1)}, f32[1280]{0:T(1024)S(1)}) all-reduce(f32[4096]{0:T(1024)S(1)} %get-tuple-element.49, f32[1280]{0:T(1024)S(1)} %get-tuple-element.51), channel_id=1, replica_groups=mesh['section_0'=2,'section_1'=8,'fsdp_0'=2,'fsdp_1'=4,'fsdp_2'=2] {'sec..., use_global_device_ids=true, to_apply=%region_18.19 | all-reduce | flops 5376 | bytes 43008 | tf_op jit(solution)/shard_map/psum | solution.py:68
  444.4 23.7 %all-reduce.1 = (f32[4096]{0:T(1024)S(1)}, f32[1280]{0:T(1024)S(1)}) all-reduce(f32[4096]{0:T(1024)S(1)} %get-tuple-element.62, f32[1280]{0:T(1024)S(1)} %get-tuple-element.63), channel_id=1, replica_groups=mesh['section_0'=2,'section_1'=8,'fsdp_0'=2,'fsdp_1'=4,'fsdp_2'=2] {'sec..., use_global_device_ids=true, to_apply=%region_19.20 | all-reduce | flops 5376 | bytes 43008 | tf_op jit(solution)/shard_map/psum | solution.py:68
  468.1 6.1 %all-reduce.4 = (f32[4096]{0:T(1024)S(1)}, f32[1280]{0:T(1024)S(1)}) all-reduce(f32[4096]{0:T(1024)S(1)} %get-tuple-element.54, f32[1280]{0:T(1024)S(1)} %get-tuple-element.55), channel_id=1, replica_groups=mesh['section_0'=2,'section_1'=8,'fsdp_0'=2,'fsdp_1'=4,'fsdp_2'=2] {'fsd..., use_global_device_ids=true, to_apply=%region_20.21 | all-reduce | flops 5376 | bytes 43008 | tf_op jit(solution)/shard_map/psum | solution.py:68
  474.2 12.4 %all-reduce.2 = (f32[4096]{0:T(1024)S(1)}, f32[1280]{0:T(1024)S(1)}) all-reduce(f32[4096]{0:T(1024)S(1)} %get-tuple-element.60, f32[1280]{0:T(1024)S(1)} %get-tuple-element.61), channel_id=1, replica_groups=mesh['section_0'=2,'section_1'=8,'fsdp_0'=2,'fsdp_1'=4,'fsdp_2'=2] {'fsd..., use_global_device_ids=true, to_apply=%region_21.22 | all-reduce | flops 5376 | bytes 43008 | tf_op jit(solution)/shard_map/psum | solution.py:68
  486.6 19.2 %all-reduce.3 = (f32[4096]{0:T(1024)}, f32[1280]{0:T(1024)}) all-reduce(f32[4096]{0:T(1024)S(1)} %get-tuple-element.56, f32[1280]{0:T(1024)S(1)} %get-tuple-element.57), channel_id=1, replica_groups=mesh['section_0'=2,'section_1'=8,'fsdp_0'=2,'fsdp_1'=4,'fsdp_2'=2] {'fsd..., use_global_device_ids=true, to_apply=%region_22.23 | all-reduce | flops 5376 | bytes 43008 | tf_op jit(solution)/shard_map/psum | solution.py:68
  505.8 1.7 bitcast_convert_fusion
  507.5 0.9 convert_reduce_fusion.1
  508.4 1.7 slice_bitcast_fusion
  (69 shorter events, 1.9 us)
Async XLA Ops:
  7.2 11.7 %copy-start.6 = (bf16[1,128,640]{2,1,0:T(8,128)(2,1)S(1)}, bf16[1,128,640]{2,1,0:T(8,128)(2,1)}, u32[]{:S(2)}) copy-start(bf16[1,128,640]{2,1,0:T(8,128)(2,1)} %param.13) | copy-start | bytes 491524
  7.2 11.9 %copy-start.11 = (s32[1,4]{1,0:T(1,128)S(1)}, s32[1,4]{1,0:T(1,128)}, u32[]{:S(2)}) copy-start(s32[1,4]{1,0:T(1,128)} %param.16) | copy-start | bytes 52
  7.2 60.0 %all-gather.5.cloned.1.call-start = ((), (), s32[]{:S(2)}) async-start(), calls=%async_computation.9 | async-start | bytes 5570560 | tf_op jit(solution)/shard_map/all_gather | solution.py:17
  9.0 147.4 %all-gather.9.cloned.1.call-start = ((), (), s32[]{:S(2)}) async-start(), calls=%async_computation.11 | async-start | bytes 2785280 | tf_op jit(solution)/shard_map/all_gather | solution.py:150
  12.0 83.5 %all-to-all-start = ((bf16[16,40,1280]{2,1,0:T(8,128)(2,1)}), bf16[16,40,1280]{2,1,0:T(8,128)(2,1)S(1)}, u32[]{:S(2)}, u32[]{:S(2)}) async-start(bf16[16,40,1280]{2,1,0:T(8,128)(2,1)} %broadcast_in_dim.74), calls=%async_computation | async-start | bytes 3276800 | tf_op jit(solution)/shard_map/all_to_all | solution.py:29
  18.8 182.6 %all-gather.7.cloned.1.call-start = ((), (), s32[]{:S(2)}) async-start(), calls=%async_computation.10 | async-start | bytes 5570560 | tf_op jit(solution)/shard_map/all_gather | solution.py:147
  19.0 62.5 %copy-start.7 = (bf16[1,128,640]{1,2,0:T(8,128)(2,1)}, bf16[1,128,640]{1,2,0:T(8,128)(2,1)S(1)}, u32[]{:S(2)}) copy-start(bf16[1,128,640]{1,2,0:T(8,128)(2,1)S(1)} %copy.73) | copy-start | bytes 491524
  90.2 6.5 %copy-start.5 = (bf16[1,128,1280]{2,1,0:T(8,128)(2,1)S(1)}, bf16[1,128,1280]{2,1,0:T(8,128)(2,1)}, u32[]{:S(2)}) copy-start(bf16[1,128,1280]{2,1,0:T(8,128)(2,1)} %param.12) | copy-start | bytes 983044
  90.2 8.7 %copy-start.9 = (f32[1280]{0:T(1024)S(1)}, f32[1280]{0:T(1024)}, u32[]{:S(2)}) copy-start(f32[1280]{0:T(1024)} %param.19) | copy-start | bytes 15364
  95.4 4.6 copy-start.13
  95.4 5.9 %copy-start.12 = (s32[1,32]{1,0:T(1,128)S(1)}, s32[1,32]{1,0:T(1,128)}, u32[]{:S(2)}) copy-start(s32[1,32]{1,0:T(1,128)} %param.17) | copy-start | bytes 388
  95.4 1.2 copy-start.1
  206.2 13.8 %copy-start = (bf16[1,128,4096]{2,1,0:T(8,128)(2,1)S(1)}, bf16[1,128,4096]{2,1,0:T(8,128)(2,1)}, u32[]{:S(2)}) copy-start(bf16[1,128,4096]{2,1,0:T(8,128)(2,1)} %param.21) | copy-start | bytes 3145732
  208.8 11.1 %all-to-all-start.1 = ((bf16[16,32,256]{2,1,0:T(8,128)(2,1)}), bf16[16,32,256]{2,1,0:T(8,128)(2,1)S(1)}, u32[]{:S(2)}, u32[]{:S(2)}) async-start(bf16[16,32,256]{2,1,0:T(8,128)(2,1)} %bitcast.15), calls=%async_computation.1 | async-start | bytes 524288 | tf_op jit(solution)/shard_map/all_to_all | solution.py:157
  212.5 9.5 %copy-start.2 = (bf16[1,128,4096]{2,1,0:T(8,128)(2,1)S(1)}, bf16[1,128,4096]{2,1,0:T(8,128)(2,1)}, u32[]{:S(2)}) copy-start(bf16[1,128,4096]{2,1,0:T(8,128)(2,1)} %param.23) | copy-start | bytes 3145732
  212.5 9.5 %copy-start.10 = (f32[4096]{0:T(1024)S(1)}, f32[4096]{0:T(1024)}, u32[]{:S(2)}) copy-start(f32[4096]{0:T(1024)} %param.22) | copy-start | bytes 49156
  221.7 2.2 copy-start.3
  225.9 12.9 %all-to-all-start.2 = ((bf16[32,16,256]{2,0,1:T(8,128)(2,1)}), bf16[32,16,256]{2,0,1:T(8,128)(2,1)S(1)}, u32[]{:S(2)}, u32[]{:S(2)}) async-start(bf16[32,16,256]{2,0,1:T(8,128)(2,1)} %bitcast.92), calls=%async_computation.2 | async-start | bytes 524288 | tf_op jit(solution)/shard_map/all_to_all | solution.py:173
  246.5 74.8 %all-to-all-start.3 = ((bf16[16,32,5120]{2,1,0:T(8,128)(2,1)}), bf16[16,32,5120]{2,1,0:T(8,128)(2,1)}, u32[]{:S(2)}, u32[]{:S(2)}) async-start(bf16[16,32,5120]{2,1,0:T(8,128)(2,1)} %bitcast.95), calls=%async_computation.3 | async-start | bytes 10485760 | tf_op jit(solution)/shard_map/all_to_all | solution.py:44
  251.5 111.4 %reduce-scatter.6.cloned.1.call-start = ((), (), s32[]{:S(2)}) async-start(), calls=%async_computation.13 | async-start | bytes 2949120 | tf_op jit(solution)/shard_map/reduce_scatter | solution.py:53
  257.3 248.5 %reduce-scatter.8.cloned.1.call-start = ((), (), s32[]{:S(2)}) async-start(), calls=%async_computation.14 | async-start | bytes 491520 | tf_op jit(solution)/shard_map/reduce_scatter | solution.py:53
  325.5 42.0 %copy-start.4 = (bf16[128,1280]{1,0:T(8,128)(2,1)}, bf16[128,1280]{1,0:T(8,128)(2,1)S(1)}, u32[]{:S(2)}) copy-start(bf16[128,1280]{1,0:T(8,128)(2,1)S(1)} %multiply_convert_fusion.1) | copy-start | bytes 983044
  337.5 6.4 %copy-start.8 = (bf16[1,128,640]{1,2,0:T(8,128)(2,1)S(1)}, bf16[1,128,640]{1,2,0:T(8,128)(2,1)}, u32[]{:S(2)}) copy-start(bf16[1,128,640]{1,2,0:T(8,128)(2,1)} %copy-done.7) | copy-start | bytes 491524
  363.0 145.5 %reduce-scatter.4.cloned.1.call-start = ((), (), s32[]{:S(2)}) async-start(), calls=%async_computation.12 | async-start | bytes 5570560 | tf_op jit(solution)/shard_map/reduce_scatter | solution.py:79
  398.5 109.0 %all-to-all-start.5 = ((bf16[16,40,1280]{2,1,0:T(8,128)(2,1)}), bf16[16,40,1280]{2,1,0:T(8,128)(2,1)S(1)}, u32[]{:S(2)}, u32[]{:S(2)}) async-start(bf16[16,40,1280]{2,1,0:T(8,128)(2,1)} %broadcast_in_dim.80), calls=%async_computation.8 | async-start | bytes 3276800 | tf_op jit(solution)/shard_map/all_to_all | solution.py:29
Sparse Core Ops, SparseCore 0:
  10.4 56.7 all-gather.4
  69.8 86.6 all-gather.8
  158.9 42.4 all-gather.6
  257.5 41.4 reduce-scatter.5
  363.1 36.0 reduce-scatter.7
  401.6 71.8 reduce-scatter.3
where the time goes:
time: 518 us; the launch traced here: 517 us
  waiting for transfers between devices  207 us (40%)
  blocking collectives  120 us (23%)
  matrix products  75.3 us (15%)
  local copies, waits for them, and re-layouts  44.2 us (9%)
  starting transfers between devices  31 us (6%)
  other arithmetic  24.6 us (5%)
  between operations  15.2 us (3%)
    psum x5, blocking collectives, over_axes(): x = lax.psum(x, axis)  82.7 us
    all_to_all x1, waiting for transfers between devices, sum_at_owner(): lax.all_to_all(pieces, axis, split_axis=0, concat_axis=0, tiled=True)  63.6 us
    all_gather x1, waiting for transfers between devices, sent_together(): result = lax.all_gather(both, axis, axis=dim, tiled=True)  47.4 us
    all_gather x1, waiting for transfers between devices, on_device(): lax.all_gather(merged_local, FSDP, axis=0, tiled=True)  44.9 us
    all_gather x1, waiting for transfers between devices, on_device(): merger_cols = lax.all_gather(merger_weight, SECTION, axis=0, tiled=True)  42.9 us
    all_to_all x1, blocking collectives, sum_at_owner(): lax.all_to_all(pieces, axis, split_axis=0, concat_axis=0, tiled=True)  28.9 us
    all_to_all x2, starting transfers between devices, sent_to_all(): return lax.all_to_all(copies, axis, split_axis=0, concat_axis=0, tiled=True)  16 us
    dot_general x1, matrix products, on_device(): jnp.einsum('hqk,khd->qhd', score_low, key_heads, preferred_element_type=j...  14.6 us
  transfers between devices with their start and end apart: 11, of which 5 were waited for; matrix products, arithmetic and copies ran while one was open for 23% of the time, Pallas kernels for 0%

commit v1 on v0

--- a/solution.py
+++ b/solution.py
@@ -9,6 +9,12 @@
 SECTION = ("section_0", "section_1")
 SECTION_FSDP = ("section_0", "section_1", "fsdp_0", "fsdp_1", "fsdp_2")
 EPS = 1e-06
+
+
+def gather_and_add(value, axis):
+    parts = lax.all_gather(value, axis, axis=0, tiled=False)
+    total = parts.sum(axis=0)
+    return total
 
 
 def sent_together(arrays, axis, dim, along):
@@ -65,7 +71,7 @@
 
 def over_axes(x, axes):
     for axis in axes:
-        x = lax.psum(x, axis)
+        x = gather_and_add(x, axis)
     return x
 
 

time: 518 us -> 565 us (1.091)
  blocking collectives: 120 us -> 166 us
    all_gather x0 -> x10, blocking collectives: none -> 128 us  [gather_and_add(): parts = lax.all_gather(value, axis, axis=0, tiled=False)]
    psum x5 -> x0, blocking collectives: 82.7 us -> none  [over_axes(): x = lax.psum(x, axis)]
  transfers between devices with their start and end apart: 11 -> 11, of which waited for: 5 -> 5; matrix products, arithmetic and copies ran while one was open for 23% -> 21% of each run, Pallas kernels for 0% -> 0%
where the time goes in v1:
time: 565 us; the launch traced here: 564 us
  waiting for transfers between devices  207 us (37%)
  blocking collectives  166 us (29%)
  matrix products  75 us (13%)
  local copies, waits for them, and re-layouts  44.3 us (8%)
  starting transfers between devices  31 us (5%)
  other arithmetic  26.1 us (5%)
  between operations  15.3 us (3%)
    all_gather x10, blocking collectives, gather_and_add(): parts = lax.all_gather(value, axis, axis=0, tiled=False)  128 us
    all_to_all x1, waiting for transfers between devices, sum_at_owner(): lax.all_to_all(pieces, axis, split_axis=0, concat_axis=0, tiled=True)  63.6 us
    all_gather x1, waiting for transfers between devices, sent_together(): result = lax.all_gather(both, axis, axis=dim, tiled=True)  47.4 us
    all_gather x1, waiting for transfers between devices, on_device(): lax.all_gather(merged_local, FSDP, axis=0, tiled=True)  44.9 us
    all_gather x1, waiting for transfers between devices, on_device(): merger_cols = lax.all_gather(merger_weight, SECTION, axis=0, tiled=True)  42.9 us
    all_to_all x1, blocking collectives, sum_at_owner(): lax.all_to_all(pieces, axis, split_axis=0, concat_axis=0, tiled=True)  28.9 us
    all_to_all x2, starting transfers between devices, sent_to_all(): return lax.all_to_all(copies, axis, split_axis=0, concat_axis=0, tiled=True)  16 us
    dot_general x1, matrix products, on_device(): jnp.einsum('hqk,qhd->khd', score_low, query_heads, preferred_element_type...  14.6 us
  transfers between devices with their start and end apart: 11, of which 5 were waited for; matrix products, arithmetic and copies ran while one was open for 21% of the time, Pallas kernels for 0%

profile of v1, /device:TPU:1, one launch (start us, length us, event | category | flops | bytes accessed | tf_op | source)
XLA Modules:
  0.0 564.0 jit_solution(14912115827514581697)
XLA Ops:
  7.2 1.8 pad_maximum_fusion.1
  9.1 0.7 all-gather.24.cloned.1.call-update
  9.8 2.2 broadcast_in_dim.74
  12.0 6.8 %all-to-all-start = ((bf16[16,40,1280]{2,1,0:T(8,128)(2,1)}), bf16[16,40,1280]{2,1,0:T(8,128)(2,1)S(1)}, u32[]{:S(2)}, u32[]{:S(2)}) async-start(bf16[16,40,1280]{2,1,0:T(8,128)(2,1)} %broadcast_in_dim.74), calls=%async_computation | async-start | bytes 3276800 | tf_op jit(solution)/shard_map/all_to_all | solution.py:35
  19.8 47.4 %all-gather.20.cloned.1.call-done = bf16[2048,1280]{1,0:T(8,128)(2,1)} async-done(((bf16[128,1280]{1,0:T(8,128)(2,1)}), bf16[2048,1280]{1,0:T(8,128)(2,1)}) %all-gather.20.cloned.1.call-update) | async-done | bytes 5242896 | tf_op jit(solution)/shard_map/all_gather | solution.py:23
  67.2 5.3 fusion.48
  72.5 4.6 copy.72
  77.0 4.5 copy.71
  81.5 8.7 %fusion.49 = (f32[8,128]{1,0:T(8,128)S(1)}, f32[8,128,2048]{1,2,0:T(8,128)}) fusion(pred[128,2048]{0,1:T(8,128)(4,1)S(1)} %broadcast_compare_fusion, bf16[2048,8,80]{0,2,1:T(8,128)(2,1)} %bitcast.104, bf16[128,8,80]{0,2,1:T(8,128)(2,1)S(1)} %bitcast.118), kind=kOutput, calls=%fused_computation.96 | convolution fusion | flops 346032128 | bytes 11440128 | tf_op jit(solution)/shard_map/sub | solution.py:106
  90.2 5.2 fusion.30
  95.4 1.2 copy-done.1
  96.7 2.0 fusion.50
  99.1 0.9 reshape.203
  100.0 0.6 dynamic-slice
  101.4 8.4 %all-reduce = s32[512]{0:T(512)S(1)} all-reduce(s32[512]{0:T(512)S(1)} %bitcast_dynamic-update-slice_fusion), channel_id=2, replica_groups=mesh['section_0'=2,'section_1'=8,'fsdp_0'=2,'fsdp_1'=4,'fsdp_2'=2] {'fsd..., use_global_device_ids=true, to_apply=%add | all-reduce | flops 512 | bytes 4096 | tf_op jit(solution)/shard_map/all_gather | solution.py:154
  109.8 3.8 sort.31
  113.6 42.9 %all-gather.24.cloned.1.call-done = bf16[5120,256]{1,0:T(8,128)(2,1)} async-done(((bf16[320,256]{1,0:T(8,128)(2,1)}), bf16[5120,256]{1,0:T(8,128)(2,1)}) %all-gather.24.cloned.1.call-update) | async-done | bytes 2621456 | tf_op jit(solution)/shard_map/all_gather | solution.py:156
  156.5 44.9 %all-gather.22.cloned.1.call-done = bf16[512,5120]{1,0:T(8,128)(2,1)} async-done(((bf16[32,5120]{1,0:T(8,128)(2,1)}), bf16[512,5120]{1,0:T(8,128)(2,1)}) %all-gather.22.cloned.1.call-update) | async-done | bytes 5242896 | tf_op jit(solution)/shard_map/all_gather | solution.py:153
  201.4 4.8 convolution_convert_fusion.4
  206.2 2.6 gather_fusion.1
  208.8 3.8 all-to-all-start.1
  212.6 3.5 gather_fusion
  216.1 3.8 sort.32
  220.0 1.7 scatter_fusion
  222.0 1.8 fusion.26
  223.9 0.6 fusion.22
  224.5 0.7 gather_fusion.2
  225.2 0.7 copy.95
  225.9 5.7 %all-to-all-start.2 = ((bf16[32,16,256]{2,0,1:T(8,128)(2,1)}), bf16[32,16,256]{2,0,1:T(8,128)(2,1)S(1)}, u32[]{:S(2)}, u32[]{:S(2)}) async-start(bf16[32,16,256]{2,0,1:T(8,128)(2,1)} %bitcast.92), calls=%async_computation.2 | async-start | bytes 524288 | tf_op jit(solution)/shard_map/all_to_all | solution.py:179
  231.6 7.2 %all-to-all-done.2 = bf16[32,16,256]{2,0,1:T(8,128)(2,1)S(1)} async-done(((bf16[32,16,256]{2,0,1:T(8,128)(2,1)}), bf16[32,16,256]{2,0,1:T(8,128)(2,1)S(1)}, u32[]{:S(2)}, u32[]{:S(2)}) %all-to-all-start.2) | async-done | bytes 262176 | tf_op jit(solution)/shard_map/all_to_all | solution.py:179
  238.8 1.9 gather_fusion.3
  240.8 5.7 %convolution_convert_fusion = bf16[512,5120]{1,0:T(8,128)(2,1)} fusion(bf16[512,256]{1,0:T(8,128)(2,1)S(1)} %gather_fusion.3, bf16[5120,256]{1,0:T(8,128)(2,1)} %all-gather.24.cloned.1.call-done), kind=kOutput, calls=%fused_computation.13 | convolution fusion | flops 1344798720 | bytes 8126464 | tf_op jit(solution)/shard_map/dot_general | solution.py:182
  246.5 5.1 all-to-all-start.3
  251.6 4.1 convolution_convert_fusion.1
  255.7 1.7 copy.85
  257.6 63.6 %all-to-all-done.3 = bf16[16,32,5120]{2,1,0:T(8,128)(2,1)} async-done(((bf16[16,32,5120]{2,1,0:T(8,128)(2,1)}), bf16[16,32,5120]{2,1,0:T(8,128)(2,1)}, u32[]{:S(2)}, u32[]{:S(2)}) %all-to-all-start.3) | async-done | bytes 5242912 | tf_op jit(solution)/shard_map/all_to_all | solution.py:50
  321.2 3.5 convert_reduce_fusion
  325.5 2.2 convolution_convert_fusion.5
  327.9 6.5 %convolution_convert_fusion.3 = bf16[8,80,2048]{2,1,0:T(8,128)(2,1)} fusion(bf16[128,8,80]{0,2,1:T(8,128)(2,1)S(1)} %bitcast.114, f32[8,128,2048]{1,2,0:T(8,128)} %get-tuple-element.60, f32[8,128]{1,0:T(8,128)S(1)} %get-tuple-element.59), kind=kOutput, calls=%fused_computation.26 | convolution fusion | flops 341049344 | bytes 11177984 | tf_op jit(solution)/shard_map/hqk,qhd->khd/dot_general | solution.py:217
  334.4 3.1 copy.84
  337.5 6.4 %fusion.51 = f32[8,128,2048]{1,2,0:T(8,128)} fusion(bf16[128,8,80]{0,2,1:T(8,128)(2,1)S(1)} %bitcast.115, bf16[2048,8,80]{0,2,1:T(8,128)(2,1)} %bitcast.101), kind=kOutput, calls=%fused_computation.98 | convolution fusion | flops 335544320 | bytes 11173888 | tf_op jit(solution)/shard_map/qhd,khd->hqk/dot_general | solution.py:220
  344.0 14.6 %fusion.15 = bf16[8,2048,80]{1,2,0:T(8,128)(2,1)} fusion(bf16[128,8,80]{0,2,1:T(8,128)(2,1)S(1)} %bitcast.119, f32[8,128,2048]{1,2,0:T(8,128)} %fusion.51, f32[8,128,2048]{1,2,0:T(8,128)} %get-tuple-element.60, f32[8,128]{1,0:T(8,128)S(1)} %get-tuple-element.59), kind=kOutput, calls=%fused_computation.24 | convolution fusion | flops 351538176 | bytes 19566592 | tf_op jit(solution)/shard_map/hqk,qhd->khd/dot_general | solution.py:228
  358.6 4.4 copy.83
  363.0 4.4 pad_maximum_fusion
  368.1 28.9 %all_to_all.55 = bf16[16,40,1280]{2,1,0:T(8,128)(2,1)S(1)} all-to-all(bf16[16,40,1280]{2,1,0:T(8,128)(2,1)S(1)} %bitcast.102), channel_id=1, replica_groups=mesh['section_0'=2,'section_1'=8,'fsdp_0'=2,'fsdp_1'=4,'fsdp_2'=2] {'fsd..., dimensions={0} | all-to-all | bytes 3276800 | tf_op jit(solution)/shard_map/all_to_all | solution.py:50
  397.2 1.3 broadcast_in_dim.80
  398.5 9.2 %all-to-all-start.5 = ((bf16[16,40,1280]{2,1,0:T(8,128)(2,1)}), bf16[16,40,1280]{2,1,0:T(8,128)(2,1)S(1)}, u32[]{:S(2)}, u32[]{:S(2)}) async-start(bf16[16,40,1280]{2,1,0:T(8,128)(2,1)} %broadcast_in_dim.80), calls=%async_computation.8 | async-start | bytes 3276800 | tf_op jit(solution)/shard_map/all_to_all | solution.py:35
  407.7 5.7 %all-gather.1 = f32[8192]{0:T(1024)S(1)} all-gather(f32[4096]{0:T(1024)S(1)} %get-tuple-element.49), channel_id=3, replica_groups=mesh['section_0'=2,'section_1'=8,'fsdp_0'=2,'fsdp_1'=4,'fsdp_2'=2] {'sec..., dimensions={0}, use_global_device_ids=true | all-gather | bytes 49152 | tf_op jit(solution)/shard_map/all_gather | solution.py:15
  413.5 52.0 %all-gather.2 = f32[32768]{0:T(1024)S(1)} all-gather(f32[4096]{0:T(1024)S(1)} %reduce_sum.240), channel_id=4, replica_groups=mesh['section_0'=2,'section_1'=8,'fsdp_0'=2,'fsdp_1'=4,'fsdp_2'=2] {'sec..., dimensions={0}, use_global_device_ids=true | all-gather | bytes 147456 | tf_op jit(solution)/shard_map/all_gather | solution.py:15
  465.6 4.0 all-gather.3
  469.6 9.2 %all-gather.4 = f32[16384]{0:T(1024)S(1)} all-gather(f32[4096]{0:T(1024)S(1)} %reduce_sum.242), channel_id=6, replica_groups=mesh['section_0'=2,'section_1'=8,'fsdp_0'=2,'fsdp_1'=4,'fsdp_2'=2] {'fsd..., dimensions={0}, use_global_device_ids=true | all-gather | bytes 81920 | tf_op jit(solution)/shard_map/all_gather | solution.py:15
  478.9 8.2 %all-gather.5 = f32[8192]{0:T(1024)S(1)} all-gather(f32[4096]{0:T(1024)S(1)} %reduce_sum.243), channel_id=7, replica_groups=mesh['section_0'=2,'section_1'=8,'fsdp_0'=2,'fsdp_1'=4,'fsdp_2'=2] {'fsd..., dimensions={0}, use_global_device_ids=true | all-gather | bytes 49152 | tf_op jit(solution)/shard_map/all_gather | solution.py:15
  487.2 0.6 reduce_sum.244
  487.8 4.7 all-gather.11
  492.6 18.4 %all-gather.12 = f32[8,1,1280]{2,1,0:T(1,128)S(1)} all-gather(f32[1,1,1280]{2,1,0:T(1,128)S(1)} %reshape.273), channel_id=9, replica_groups=mesh['section_0'=2,'section_1'=8,'fsdp_0'=2,'fsdp_1'=4,'fsdp_2'=2] {'sec..., dimensions={0}, use_global_device_ids=true | all-gather | bytes 46080 | tf_op jit(solution)/shard_map/all_gather | solution.py:15
  511.0 3.2 all-gather.13
  514.3 9.1 %all-gather.14 = f32[4,1,1280]{2,1,0:T(1,128)S(1)} all-gather(f32[1,1,1280]{2,1,0:T(1,128)S(1)} %reshape.277), channel_id=11, replica_groups=mesh['section_0'=2,'section_1'=8,'fsdp_0'=2,'fsdp_1'=4,'fsdp_2'=2] {'fsd..., dimensions={0}, use_global_device_ids=true | all-gather | bytes 25600 | tf_op jit(solution)/shard_map/all_gather | solution.py:15
  523.4 13.6 %all-gather.15 = f32[2,1,1280]{2,1,0:T(1,128)S(1)} all-gather(f32[1,1,1280]{2,1,0:T(1,128)S(1)} %reshape.279), channel_id=12, replica_groups=mesh['section_0'=2,'section_1'=8,'fsdp_0'=2,'fsdp_1'=4,'fsdp_2'=2] {'fsd..., dimensions={0}, use_global_device_ids=true | all-gather | bytes 15360 | tf_op jit(solution)/shard_map/all_gather | solution.py:15
  537.1 0.6 reduce_sum.250
  537.7 14.3 %fusion.33 = bf16[8,80,128]{2,1,0:T(8,128)(2,1)S(1)} fusion(bf16[2048,8,80]{0,2,1:T(8,128)(2,1)} %bitcast.105, f32[8,128,2048]{1,2,0:T(8,128)} %fusion.51, f32[8,128,2048]{1,2,0:T(8,128)} %get-tuple-element.60, f32[8,128]{1,0:T(8,128)S(1)} %get-tuple-element.59), kind=kOutput, calls=%fused_computation.46 | convolution fusion | flops 350309376 | bytes 19566592 | tf_op jit(solution)/shard_map/hqk,khd->qhd/dot_general | solution.py:225
  552.0 0.8 copy.86
  552.8 1.7 bitcast_convert_fusion
  554.4 0.9 convert_reduce_fusion.1
  555.4 1.7 slice_bitcast_fusion
  (94 shorter events, 4.6 us)
Async XLA Ops:
  7.2 11.7 %copy-start.6 = (bf16[1,128,640]{2,1,0:T(8,128)(2,1)S(1)}, bf16[1,128,640]{2,1,0:T(8,128)(2,1)}, u32[]{:S(2)}) copy-start(bf16[1,128,640]{2,1,0:T(8,128)(2,1)} %param.13) | copy-start | bytes 491524
  7.2 11.9 %copy-start.11 = (s32[1,4]{1,0:T(1,128)S(1)}, s32[1,4]{1,0:T(1,128)}, u32[]{:S(2)}) copy-start(s32[1,4]{1,0:T(1,128)} %param.16) | copy-start | bytes 52
  7.2 60.0 %all-gather.20.cloned.1.call-start = ((), (), s32[]{:S(2)}) async-start(), calls=%async_computation.9 | async-start | bytes 5570560 | tf_op jit(solution)/shard_map/all_gather | solution.py:23
  9.0 147.4 %all-gather.24.cloned.1.call-start = ((), (), s32[]{:S(2)}) async-start(), calls=%async_computation.11 | async-start | bytes 2785280 | tf_op jit(solution)/shard_map/all_gather | solution.py:156
  12.0 83.5 %all-to-all-start = ((bf16[16,40,1280]{2,1,0:T(8,128)(2,1)}), bf16[16,40,1280]{2,1,0:T(8,128)(2,1)S(1)}, u32[]{:S(2)}, u32[]{:S(2)}) async-start(bf16[16,40,1280]{2,1,0:T(8,128)(2,1)} %broadcast_in_dim.74), calls=%async_computation | async-start | bytes 3276800 | tf_op jit(solution)/shard_map/all_to_all | solution.py:35
  18.8 182.6 %all-gather.22.cloned.1.call-start = ((), (), s32[]{:S(2)}) async-start(), calls=%async_computation.10 | async-start | bytes 5570560 | tf_op jit(solution)/shard_map/all_gather | solution.py:153
  19.0 62.5 %copy-start.7 = (bf16[1,128,640]{1,2,0:T(8,128)(2,1)}, bf16[1,128,640]{1,2,0:T(8,128)(2,1)S(1)}, u32[]{:S(2)}) copy-start(bf16[1,128,640]{1,2,0:T(8,128)(2,1)S(1)} %copy.73) | copy-start | bytes 491524
  90.2 6.5 %copy-start.5 = (bf16[1,128,1280]{2,1,0:T(8,128)(2,1)S(1)}, bf16[1,128,1280]{2,1,0:T(8,128)(2,1)}, u32[]{:S(2)}) copy-start(bf16[1,128,1280]{2,1,0:T(8,128)(2,1)} %param.12) | copy-start | bytes 983044
  90.2 8.7 %copy-start.9 = (f32[1280]{0:T(1024)S(1)}, f32[1280]{0:T(1024)}, u32[]{:S(2)}) copy-start(f32[1280]{0:T(1024)} %param.19) | copy-start | bytes 15364
  95.4 4.6 copy-start.13
  95.4 5.9 %copy-start.12 = (s32[1,32]{1,0:T(1,128)S(1)}, s32[1,32]{1,0:T(1,128)}, u32[]{:S(2)}) copy-start(s32[1,32]{1,0:T(1,128)} %param.17) | copy-start | bytes 388
  95.4 1.2 copy-start.1
  206.2 13.8 %copy-start = (bf16[1,128,4096]{2,1,0:T(8,128)(2,1)S(1)}, bf16[1,128,4096]{2,1,0:T(8,128)(2,1)}, u32[]{:S(2)}) copy-start(bf16[1,128,4096]{2,1,0:T(8,128)(2,1)} %param.21) | copy-start | bytes 3145732
  208.8 11.1 %all-to-all-start.1 = ((bf16[16,32,256]{2,1,0:T(8,128)(2,1)}), bf16[16,32,256]{2,1,0:T(8,128)(2,1)S(1)}, u32[]{:S(2)}, u32[]{:S(2)}) async-start(bf16[16,32,256]{2,1,0:T(8,128)(2,1)} %bitcast.15), calls=%async_computation.1 | async-start | bytes 524288 | tf_op jit(solution)/shard_map/all_to_all | solution.py:163
  212.5 9.5 %copy-start.2 = (bf16[1,128,4096]{2,1,0:T(8,128)(2,1)S(1)}, bf16[1,128,4096]{2,1,0:T(8,128)(2,1)}, u32[]{:S(2)}) copy-start(bf16[1,128,4096]{2,1,0:T(8,128)(2,1)} %param.23) | copy-start | bytes 3145732
  212.5 9.5 %copy-start.10 = (f32[4096]{0:T(1024)S(1)}, f32[4096]{0:T(1024)}, u32[]{:S(2)}) copy-start(f32[4096]{0:T(1024)} %param.22) | copy-start | bytes 49156
  221.7 2.2 copy-start.3
  225.9 12.9 %all-to-all-start.2 = ((bf16[32,16,256]{2,0,1:T(8,128)(2,1)}), bf16[32,16,256]{2,0,1:T(8,128)(2,1)S(1)}, u32[]{:S(2)}, u32[]{:S(2)}) async-start(bf16[32,16,256]{2,0,1:T(8,128)(2,1)} %bitcast.92), calls=%async_computation.2 | async-start | bytes 524288 | tf_op jit(solution)/shard_map/all_to_all | solution.py:179
  246.5 74.8 %all-to-all-start.3 = ((bf16[16,32,5120]{2,1,0:T(8,128)(2,1)}), bf16[16,32,5120]{2,1,0:T(8,128)(2,1)}, u32[]{:S(2)}, u32[]{:S(2)}) async-start(bf16[16,32,5120]{2,1,0:T(8,128)(2,1)} %bitcast.95), calls=%async_computation.3 | async-start | bytes 10485760 | tf_op jit(solution)/shard_map/all_to_all | solution.py:50
  251.5 111.4 %reduce-scatter.6.cloned.1.call-start = ((), (), s32[]{:S(2)}) async-start(), calls=%async_computation.13 | async-start | bytes 2949120 | tf_op jit(solution)/shard_map/reduce_scatter | solution.py:59
  257.3 295.4 %reduce-scatter.8.cloned.1.call-start = ((), (), s32[]{:S(2)}) async-start(), calls=%async_computation.14 | async-start | bytes 491520 | tf_op jit(solution)/shard_map/reduce_scatter | solution.py:59
  325.5 42.0 %copy-start.4 = (bf16[128,1280]{1,0:T(8,128)(2,1)}, bf16[128,1280]{1,0:T(8,128)(2,1)S(1)}, u32[]{:S(2)}) copy-start(bf16[128,1280]{1,0:T(8,128)(2,1)S(1)} %multiply_convert_fusion.1) | copy-start | bytes 983044
  337.5 6.4 %copy-start.8 = (bf16[1,128,640]{1,2,0:T(8,128)(2,1)S(1)}, bf16[1,128,640]{1,2,0:T(8,128)(2,1)}, u32[]{:S(2)}) copy-start(bf16[1,128,640]{1,2,0:T(8,128)(2,1)} %copy-done.7) | copy-start | bytes 491524
  363.0 192.4 %reduce-scatter.4.cloned.1.call-start = ((), (), s32[]{:S(2)}) async-start(), calls=%async_computation.12 | async-start | bytes 5570560 | tf_op jit(solution)/shard_map/reduce_scatter | solution.py:85
  398.5 155.9 %all-to-all-start.5 = ((bf16[16,40,1280]{2,1,0:T(8,128)(2,1)}), bf16[16,40,1280]{2,1,0:T(8,128)(2,1)S(1)}, u32[]{:S(2)}, u32[]{:S(2)}) async-start(bf16[16,40,1280]{2,1,0:T(8,128)(2,1)} %broadcast_in_dim.80), calls=%async_computation.8 | async-start | bytes 3276800 | tf_op jit(solution)/shard_map/all_to_all | solution.py:35
Sparse Core Ops, SparseCore 0:
  10.4 56.7 all-gather.19
  69.8 86.6 all-gather.23
  158.9 42.4 all-gather.21
  257.5 41.4 reduce-scatter.5
  363.1 36.0 reduce-scatter.7
  401.6 71.8 reduce-scatter.3
